TPU v7x, 256 devices: a whole 4x4x8 slice. The times are simulated.
256 devices in a mesh: dp: 16 (over x, y), expert: 16 (over z, core).
Axes of the slice: x: 4, y: 4, z: 8, core: 2. Of those that a mesh axis runs over, the one named last changes fastest.
Arguments:
- tokens: bfloat16 [262144, 2048], P(('dp', 'expert')), may hold values from -16 to 16
- slot_param: bfloat16 [2048, 128], replicated, may hold values from -10 to 10
- pattern: int32 [128, 2048], P(None, ('dp', 'expert')), may hold values from 0 to 1, as said below
- w_in: bfloat16 [32, 2048, 4096], P('expert', None, 'dp'), may hold values from -0.125 to 0.125
- w_out: bfloat16 [32, 4096, 2048], P('expert', 'dp'), may hold values from -0.09375 to 0.09375
Outputs:
- mixed: bfloat16 [262144, 2048], P(('dp', 'expert'))
Inputs may be any that keep to these rules, and one draw needn't show every extreme that they name: `pattern`: every slot sees at least one block; about a quarter of all pairs are 1.
All inputs are finite; a program needn't handle non-finite values.
Results may differ from a plain program's by a relative error of at most 0.0095.
Values may be sent and summed in bfloat16 or wider, within the bound.
No kernel may reach another device: no remote copies, remote signals or barrier semaphores. Data moves between devices by JAX's collectives and lax.ppermute only.
A program may use at most 64 MiB of HBM per device.

v0:
```python
import jax
import jax.numpy as jnp
from jax import lax
from jax.sharding import PartitionSpec as P

D = 2048
EXP_DEV = 2
SLOTS = 4
BLOCK = 128
floor_value = -1e30


def local(tokens, slot_param, pattern, w_in, w_out):
    logits = jnp.dot(tokens, slot_param, preferred_element_type=jnp.float32)
    visible = jnp.repeat(pattern.T > 0, BLOCK, axis=0)
    local_peak = jnp.max(jnp.where(visible, logits, floor_value), axis=0)
    slot_peak = lax.pmax(local_peak, ("dp", "expert"))
    weights = jnp.where(visible, jnp.exp(logits - slot_peak[None, :]), 0.0).astype(jnp.bfloat16)
    weight_sum = jnp.sum(weights.astype(jnp.float32), axis=0)
    numerator = lax.dot_general(
        weights, tokens, (((0,), (0,)), ((), ())), preferred_element_type=jnp.float32
    )
    owned_num, owned_den = (
        lax.psum_scatter(numerator, "expert", scatter_dimension=0, tiled=True),
        lax.psum_scatter(weight_sum, "expert", scatter_dimension=0, tiled=True),
    )
    slot_num, slot_den = lax.psum((owned_num, owned_den), "dp")
    slot_in = (slot_num / slot_den[:, None]).astype(jnp.bfloat16)
    grouped = slot_in.reshape(EXP_DEV, SLOTS, D)
    hidden = jax.nn.gelu(
        jnp.einsum("esd,edh->esh", grouped, w_in, preferred_element_type=jnp.float32)
    ).astype(jnp.bfloat16)
    partial_value = jnp.einsum(
        "esh,ehd->esd", hidden, w_out, preferred_element_type=jnp.float32
    ).reshape(EXP_DEV * SLOTS, D)
    mixing = jax.nn.softmax(logits, axis=1).astype(jnp.bfloat16)
    owned_out = lax.psum(partial_value, "dp").astype(jnp.bfloat16)
    slot_out = lax.all_gather(owned_out, "expert", axis=0, tiled=True)
    result = jnp.dot(mixing, slot_out, preferred_element_type=jnp.float32)
    return result.astype(jnp.bfloat16)


def solution(mesh):
    return jax.shard_map(
        local,
        mesh=mesh,
        in_specs=(
            P(("dp", "expert"), None),
            P(),
            P(None, ("dp", "expert")),
            P("expert", None, "dp"),
            P("expert", "dp", None),
        ),
        out_specs=P(("dp", "expert"), None),
        check_vma=False,
    )
```

profile of v0, /device:TPU:1, one launch (start us, length us, event | category | flops | bytes accessed | tf_op | source)
XLA Modules:
  0.0 349.2 jit_solution(14017881914688491348)
XLA Ops:
  6.5 0.0 copy-start
  6.5 0.0 reduce-scatter.2.cloned.1.call-start
  6.5 0.8 compare_bitcast_fusion
  7.4 3.6 %fusion.24 = (f32[1024]{0:T(1024)S(1)}, f32[1024,128]{1,0:T(8,128)S(1)}) fusion(bf16[1024,2048]{1,0:T(8,128)(2,1)} %param.5, bf16[2048,128]{1,0:T(8,128)(2,1)} %param.6), kind=kOutput, calls=%fused_computation.31 | convolution fusion | flops 537000960 | bytes 5246976 | tf_op jit(solution)/shard_map/dot_general | solution.py:14
  11.0 0.0 copy-start.1
  11.0 0.4 fusion.2
  11.4 81.4 %pmax.7 = f32[128]{0:T(128)S(1)} all-reduce(f32[128]{0:T(128)S(1)} %get-tuple-element.6), channel_id=1, replica_groups=mesh['dp'=16,'expert'=16] {'dp','expert'}, use_global_device_ids=true, to_apply=%region_3.4 | all-reduce | flops 128 | bytes 1024 | tf_op jit(solution)/shard_map/pmax | solution.py:17
  92.8 0.2 convert_reduce_fusion
  92.9 3.9 %fusion.27 = f32[128,2048]{1,0:T(8,128)} fusion(bf16[1024,128]{1,0:T(8,128)(2,1)S(1)} %get-tuple-element.8, bf16[1024,2048]{1,0:T(8,128)(2,1)} %param.5), kind=kOutput, calls=%fused_computation.33 | convolution fusion | flops 536870912 | bytes 5505024 | tf_op jit(solution)/shard_map/dot_general | solution.py:20
  96.8 0.0 reduce-scatter.2.cloned.1.call-update
  96.9 0.0 all-reduce.3.cloned.1.call-start
  96.9 50.6 %reduce-scatter.2.cloned.1.call-done = f32[8,2048]{1,0:T(8,128)} async-done(((f32[128,2048]{1,0:T(8,128)}), f32[8,2048]{1,0:T(8,128)}) %reduce-scatter.2.cloned.1.call-update) | async-done | bytes 65552 | tf_op jit(solution)/shard_map/reduce_scatter | solution.py:24
  147.5 0.0 all-reduce.3.cloned.1.call-update
  147.5 0.0 copy-done.1
  147.6 0.6 dynamic-slice
  148.8 26.4 %all-reduce = f32[128]{0:T(128)S(1)} all-reduce(f32[128]{0:T(128)S(1)} %get-tuple-element.7), channel_id=3, replica_groups=mesh['dp'=16,'expert'=16] {'expert'}, use_global_device_ids=true, to_apply=%region_7.8.clone | all-reduce | flops 128 | bytes 1024
  175.2 0.1 dynamic-slice.1
  175.2 33.7 %psum.22 = f32[8]{0:T(128)S(1)} all-reduce(f32[8]{0:T(128)S(1)} %dynamic-slice.1), channel_id=1, replica_groups=mesh['dp'=16,'expert'=16] {'dp'}, use_global_device_ids=true, to_apply=%region_8.9 | all-reduce | flops 8 | bytes 64 | tf_op jit(solution)/shard_map/psum | solution.py:27
  208.9 33.4 %all-reduce.3.cloned.1.call-done = f32[8,2048]{1,0:T(8,128)} async-done(((f32[8,2048]{1,0:T(8,128)}), f32[8,2048]{1,0:T(8,128)}) %all-reduce.3.cloned.1.call-update) | async-done | bytes 65552 | tf_op jit(solution)/shard_map/psum | solution.py:27
  242.4 0.9 divide_convert_fusion.2
  243.3 0.0 copy-done
  243.3 2.3 fusion.13
  245.7 58.1 %psum.23 = bf16[8,2048]{1,0:T(8,128)(2,1)S(1)} all-reduce(f32[8,2048]{1,0:T(8,128)S(1)} %reshape.15), channel_id=1, replica_groups=mesh['dp'=16,'expert'=16] {'dp'}, use_global_device_ids=true, to_apply=%region_9.10 | all-reduce | flops 16384 | bytes 98304 | tf_op jit(solution)/shard_map/psum | solution.py:37
  303.8 35.2 %all_gather.3 = bf16[128,2048]{1,0:T(8,128)(2,1)S(1)} all-gather(bf16[8,2048]{1,0:T(8,128)(2,1)S(1)} %psum.23), channel_id=1, replica_groups=mesh['dp'=16,'expert'=16] {'expert'}, dimensions={0}, use_global_device_ids=true | all-gather | bytes 557056 | tf_op jit(solution)/shard_map/all_gather | solution.py:38
  339.0 3.4 convolution_convert_fusion
  (2 shorter events, 0.1 us)
Async XLA Ops:
  6.5 236.8 %copy-start = (bf16[2,256,2048]{2,1,0:T(8,128)(2,1)S(1)}, bf16[2,256,2048]{2,1,0:T(8,128)(2,1)}, u32[]{:S(2)}) copy-start(bf16[2,256,2048]{2,1,0:T(8,128)(2,1)} %param.9) | copy-start | bytes 6291460
  6.5 141.0 %reduce-scatter.2.cloned.1.call-start = ((), (), s32[]{:S(2)}) async-start(), calls=%async_computation.1 | async-start | bytes 1114112 | tf_op jit(solution)/shard_map/reduce_scatter | solution.py:24
  11.0 136.5 %copy-start.1 = (u32[256]{0:T(256)S(1)}, u32[256]{0:T(256)}, u32[]{:S(2)}) copy-start(u32[256]{0:T(256)} %constant.22) | copy-start | bytes 3076
  96.9 145.5 %all-reduce.3.cloned.1.call-start = ((), (), s32[]{:S(2)}) async-start(), calls=%async_computation.2 | async-start | bytes 131072 | tf_op jit(solution)/shard_map/psum | solution.py:27
Sparse Core Ops, SparseCore 0:
  97.0 50.4 reduce-scatter.1
  150.7 91.6 all-reduce.2
where the time goes:
time: 350 us; the launch traced here: 349 us
  blocking collectives  235 us (67%)
  waiting for transfers between devices  84.1 us (24%)
  between operations  14.1 us (4%)
  matrix products  13.2 us (4%)
    pmax x1, blocking collectives, local(): slot_peak = lax.pmax(local_peak, ('dp', 'expert'))  81.4 us
    psum x1, blocking collectives, local(): owned_out = lax.psum(partial_value, 'dp').astype(jnp.bfloat16)  58.1 us
    reduce_scatter x1, waiting for transfers between devices, local(): lax.psum_scatter(numerator, 'expert', scatter_dimension=0, tiled=True)  50.6 us
    all_gather x1, blocking collectives, local(): slot_out = lax.all_gather(owned_out, 'expert', axis=0, tiled=True)  35.2 us
    psum x1, blocking collectives, local(): slot_num, slot_den = lax.psum((owned_num, owned_den), 'dp')  33.7 us
    psum x1, waiting for transfers between devices, local(): slot_num, slot_den = lax.psum((owned_num, owned_den), 'dp')  33.4 us
    unnamed x1, blocking collectives  26.4 us
  transfers between devices with their start and end apart: 2, of which 2 were waited for; matrix products, arithmetic and copies ran while one was open for 0% of the time, Pallas kernels for 0%

commit v1 on v0

--- a/solution.py
+++ b/solution.py
@@ -34,7 +34,7 @@
         "esh,ehd->esd", hidden, w_out, preferred_element_type=jnp.float32
     ).reshape(EXP_DEV * SLOTS, D)
     mixing = jax.nn.softmax(logits, axis=1).astype(jnp.bfloat16)
-    owned_out = lax.psum(partial_value, "dp").astype(jnp.bfloat16)
+    owned_out = jnp.sum(lax.all_gather(partial_value, "dp"), axis=0).astype(jnp.bfloat16)
     slot_out = lax.all_gather(owned_out, "expert", axis=0, tiled=True)
     result = jnp.dot(mixing, slot_out, preferred_element_type=jnp.float32)
     return result.astype(jnp.bfloat16)

time: 350 us -> 326 us (0.931)
  blocking collectives: 235 us -> 163 us
  waiting for transfers between devices: 84.1 us -> 131 us
    psum x1 -> x0, blocking collectives: 58.1 us -> none  [local(): owned_out = lax.psum(partial_value, 'dp').astype(jnp.bfloat16)]
    all_gather x0 -> x1, waiting for transfers between devices: none -> 47.1 us  [local(): lax.all_gather(partial_value, 'dp')]
    all_gather x1, blocking collectives: 35.2 us -> 21.1 us  [local(): slot_out = lax.all_gather(owned_out, 'expert', axis=0, tiled=True)]
  transfers between devices with their start and end apart: 2 -> 3, of which waited for: 2 -> 3; matrix products, arithmetic and copies ran while one was open for 0% -> 0% of each run, Pallas kernels for 0% -> 0%
where the time goes in v1:
time: 326 us
  blocking collectives  163 us (50%)
  waiting for transfers between devices  131 us (40%)
  between operations  13.8 us (4%)
  matrix products  13.2 us (4%)
  other arithmetic  3.56 us (1%)
    pmax x1, blocking collectives, local(): slot_peak = lax.pmax(local_peak, ('dp', 'expert'))  81.4 us
    reduce_scatter x1, waiting for transfers between devices, local(): lax.psum_scatter(numerator, 'expert', scatter_dimension=0, tiled=True)  50.6 us
    all_gather x1, waiting for transfers between devices, local(): lax.all_gather(partial_value, 'dp')  47.1 us
    psum x1, blocking collectives, local(): slot_num, slot_den = lax.psum((owned_num, owned_den), 'dp')  33.6 us
    psum x1, waiting for transfers between devices, local(): slot_num, slot_den = lax.psum((owned_num, owned_den), 'dp')  33.4 us
    unnamed x1, blocking collectives  26.4 us
    all_gather x1, blocking collectives, local(): slot_out = lax.all_gather(owned_out, 'expert', axis=0, tiled=True)  21.1 us
  transfers between devices with their start and end apart: 3, of which 3 were waited for; matrix products, arithmetic and copies ran while one was open for 0% of the time, Pallas kernels for 0%

profile of v1, /device:TPU:1, one launch (start us, length us, event | category | flops | bytes accessed | tf_op | source)
XLA Modules:
  0.0 325.7 jit_solution(17764910509276290061)
XLA Ops:
  6.5 0.0 copy-start
  6.5 0.0 reduce-scatter.2.cloned.1.call-start
  6.5 0.8 compare_bitcast_fusion
  7.4 3.6 %fusion.24 = (f32[1024]{0:T(1024)S(1)}, f32[1024,128]{1,0:T(8,128)S(1)}) fusion(bf16[1024,2048]{1,0:T(8,128)(2,1)} %param.5, bf16[2048,128]{1,0:T(8,128)(2,1)} %param.6), kind=kOutput, calls=%fused_computation.31 | convolution fusion | flops 537000960 | bytes 5246976 | tf_op jit(solution)/shard_map/dot_general | solution.py:14
  11.0 0.0 copy-start.1
  11.0 0.4 fusion.2
  11.4 81.4 %pmax.7 = f32[128]{0:T(128)S(1)} all-reduce(f32[128]{0:T(128)S(1)} %get-tuple-element.6), channel_id=1, replica_groups=mesh['dp'=16,'expert'=16] {'dp','expert'}, use_global_device_ids=true, to_apply=%region_3.4 | all-reduce | flops 128 | bytes 1024 | tf_op jit(solution)/shard_map/pmax | solution.py:17
  92.8 0.2 convert_reduce_fusion
  92.9 3.9 %fusion.27 = f32[128,2048]{1,0:T(8,128)} fusion(bf16[1024,128]{1,0:T(8,128)(2,1)S(1)} %get-tuple-element.8, bf16[1024,2048]{1,0:T(8,128)(2,1)} %param.5), kind=kOutput, calls=%fused_computation.33 | convolution fusion | flops 536870912 | bytes 5505024 | tf_op jit(solution)/shard_map/dot_general | solution.py:20
  96.8 0.0 reduce-scatter.2.cloned.1.call-update
  96.9 0.0 all-reduce.3.cloned.1.call-start
  96.9 50.6 %reduce-scatter.2.cloned.1.call-done = f32[8,2048]{1,0:T(8,128)} async-done(((f32[128,2048]{1,0:T(8,128)}), f32[8,2048]{1,0:T(8,128)}) %reduce-scatter.2.cloned.1.call-update) | async-done | bytes 65552 | tf_op jit(solution)/shard_map/reduce_scatter | solution.py:24
  147.5 0.0 all-reduce.3.cloned.1.call-update
  147.5 0.0 all-gather.2.cloned.1.call-start
  147.6 0.0 copy-done.1
  147.6 0.6 dynamic-slice
  148.8 26.4 %all-reduce = f32[128]{0:T(128)S(1)} all-reduce(f32[128]{0:T(128)S(1)} %get-tuple-element.7), channel_id=3, replica_groups=mesh['dp'=16,'expert'=16] {'expert'}, use_global_device_ids=true, to_apply=%region_7.8.clone | all-reduce | flops 128 | bytes 1024
  175.2 0.1 dynamic-slice.1
  175.3 33.6 %psum.15 = f32[8]{0:T(128)S(1)} all-reduce(f32[8]{0:T(128)S(1)} %dynamic-slice.1), channel_id=1, replica_groups=mesh['dp'=16,'expert'=16] {'dp'}, use_global_device_ids=true, to_apply=%region_8.9 | all-reduce | flops 8 | bytes 64 | tf_op jit(solution)/shard_map/psum | solution.py:27
  208.9 33.4 %all-reduce.3.cloned.1.call-done = f32[8,2048]{1,0:T(8,128)} async-done(((f32[8,2048]{1,0:T(8,128)}), f32[8,2048]{1,0:T(8,128)}) %all-reduce.3.cloned.1.call-update) | async-done | bytes 65552 | tf_op jit(solution)/shard_map/psum | solution.py:27
  242.4 0.9 divide_convert_fusion.2
  243.3 0.0 copy-done
  243.3 2.3 fusion.13
  245.6 0.7 all_gather_reshape.3
  246.3 0.0 all-gather.2.cloned.1.call-update
  246.3 47.1 %all-gather.2.cloned.1.call-done = f32[16,8,2048]{2,1,0:T(8,128)} async-done(((f32[1,8,2048]{2,1,0:T(8,128)}), f32[16,8,2048]{2,1,0:T(8,128)}) %all-gather.2.cloned.1.call-update) | async-done | bytes 1048592 | tf_op jit(solution)/shard_map/all_gather | solution.py:37
  293.4 1.3 reduce_sum.29
  294.7 21.1 %all_gather.7 = bf16[128,2048]{1,0:T(8,128)(2,1)S(1)} all-gather(bf16[8,2048]{1,0:T(8,128)(2,1)S(1)} %reduce_sum.29), channel_id=1, replica_groups=mesh['dp'=16,'expert'=16] {'expert'}, dimensions={0}, use_global_device_ids=true | all-gather | bytes 557056 | tf_op jit(solution)/shard_map/all_gather | solution.py:38
  315.9 3.3 %convolution_convert_fusion = bf16[1024,2048]{1,0:T(8,128)(2,1)} fusion(bf16[128,2048]{1,0:T(8,128)(2,1)S(1)} %all_gather.7, f32[1024,128]{1,0:T(8,128)S(1)} %get-tuple-element.10, f32[1024]{0:T(1024)S(1)} %get-tuple-element.5, f32[1024]{0:T(1024)S(1)} %get-tuple-element.9), kind=kOutput, calls=%fused_computation | convolution fusion | flops 539361280 | bytes 5251072 | tf_op jit(solution)/shard_map/dot_general | solution.py:39
  (1 shorter events, 0.0 us)
Async XLA Ops:
  6.5 236.8 %copy-start = (bf16[2,256,2048]{2,1,0:T(8,128)(2,1)S(1)}, bf16[2,256,2048]{2,1,0:T(8,128)(2,1)}, u32[]{:S(2)}) copy-start(bf16[2,256,2048]{2,1,0:T(8,128)(2,1)} %param.9) | copy-start | bytes 6291460
  6.5 141.0 %reduce-scatter.2.cloned.1.call-start = ((), (), s32[]{:S(2)}) async-start(), calls=%async_computation.1 | async-start | bytes 1114112 | tf_op jit(solution)/shard_map/reduce_scatter | solution.py:24
  11.0 136.6 %copy-start.1 = (u32[256]{0:T(256)S(1)}, u32[256]{0:T(256)}, u32[]{:S(2)}) copy-start(u32[256]{0:T(256)} %constant.22) | copy-start | bytes 3076
  96.9 145.5 %all-reduce.3.cloned.1.call-start = ((), (), s32[]{:S(2)}) async-start(), calls=%async_computation.2 | async-start | bytes 131072 | tf_op jit(solution)/shard_map/psum | solution.py:27
  147.5 145.9 %all-gather.2.cloned.1.call-start = ((), (), s32[]{:S(2)}) async-start(), calls=%async_computation.3 | async-start | bytes 1114112 | tf_op jit(solution)/shard_map/all_gather | solution.py:37
Sparse Core Ops, SparseCore 0:
  97.0 50.4 reduce-scatter.1
  150.7 91.6 all-reduce.2
  246.5 46.9 all-gather.1
